TPU v7x, 512 devices: a whole 4x4x16 slice. The times are simulated.
512 devices in a mesh: req: 128 (over x, z, core), tp: 4 (over y).
Axes of the slice: x: 4, y: 4, z: 16, core: 2. Of those that a mesh axis runs over, the one named last changes fastest.
Arguments:
- queries: bfloat16 [2, 128, 32, 1536], P(None, 'req', None, 'tp')
- response_kv: bfloat16 [2, 128, 2, 32, 256], P(None, 'req'), may hold values from -6 to 6
- cache_kv: bfloat16 [2, 128, 2, 384, 256], P(None, 'req'), may hold values from -6 to 6
- residual: bfloat16 [2, 128, 32, 1536], P(None, 'req')
- out_proj: bfloat16 [2, 1536, 1536], P(None, 'tp'), may hold values from -0.5 to 0.5
- norm_gain: float32 [2, 1536], replicated, may hold values from 0.25 to 1.75
- lm_head: bfloat16 [2, 131072, 1536], P(None, 'req', 'tp')
- targets: int32 [128, 32], P(None, 'tp'), may hold values from 0 to 131071
- resp_lengths: int32 [128], replicated, may hold values from 1 to 32, 2560 in all
- cache_lengths: int32 [128], P('req'), may hold values from 1 to 384, 30720 in all
- owner_slot: int32 [128], replicated, may hold values from 0 to 127, each once
- sink_count: int32 [1], replicated, may hold values from 1 to 95
- window_size: int32 [1], replicated, may hold values from 48 to 191
Outputs:
- token_logprobs: float32 [128, 32], P('req', 'tp')
- request_scores: float32 [128, 2], P('req')
Inputs may be any that keep to these rules, and one draw needn't show every extreme that they name: `resp_lengths`: live response slots are the first ones; all lengths sum to 2560. `cache_lengths`: live cache slots are the first ones; all lengths sum to 30720. `owner_slot`: A permutation of the requests.
All inputs are finite; a program needn't handle non-finite values. No bound on the sum of `cache_lengths` on one device may be relied on, other than what follows from the above.
Results may differ from a plain program's by a relative error of at most 0.0014.
Values may be sent and summed in bfloat16 or wider, within the bound.
A program may use at most 128 MiB of HBM per device.

v0:
```python
import jax
import jax.numpy as jnp
from jax import lax
from jax.sharding import PartitionSpec as P

HEADS = 12
HEAD = 128
KV_HEADS = 2
RESP = 32
CACHE = 384


def span_mask(lengths, sink_count, window_size):
    cache_pos = jnp.arange(CACHE, dtype=jnp.int32)
    slot_pos = jnp.arange(RESP, dtype=jnp.int32)
    req_count = lengths.shape[0]
    key_pos = jnp.concatenate([cache_pos[None, :], lengths[:, None] + slot_pos[None, :]], axis=1)
    key_live = jnp.concatenate(
        [cache_pos[None, :] < lengths[:, None], jnp.ones((req_count, RESP), jnp.bool_)], axis=1
    )
    query_pos = lengths[:, None] + slot_pos[None, :]
    earlier = key_pos[:, None, :] <= query_pos[:, :, None]
    inside = (key_pos[:, None, :] < sink_count[0]) | (
        query_pos[:, :, None] - key_pos[:, None, :] < window_size[0]
    )
    return key_live[:, None, :] & earlier & inside


def rms_norm(hidden, norm_gain):
    scale_inv = lax.rsqrt(jnp.mean(hidden * hidden, axis=-1, keepdims=True) + 1e-06)
    return (hidden * scale_inv * norm_gain[:, None, None, :]).astype(jnp.bfloat16)


def per_device(
    queries,
    response_kv,
    cache_kv,
    residual,
    out_proj,
    norm_gain,
    lm_head,
    targets,
    resp_lengths,
    cache_lengths,
    owner_slot,
    sink_count,
    window_size,
):
    tp_size = lax.axis_size("tp")
    tp_index = lax.axis_index("tp")
    req_index = lax.axis_index("req")
    local_reqs = queries.shape[1]
    local_heads = HEADS // tp_size
    group_size = HEADS // KV_HEADS
    kv_index = tp_index * local_heads // group_size
    quarter = RESP // tp_size
    cache_head = lax.dynamic_slice_in_dim(cache_kv, kv_index * HEAD, HEAD, axis=4)
    resp_head = lax.dynamic_slice_in_dim(response_kv, kv_index * HEAD, HEAD, axis=4)
    key_rows = jnp.concatenate([cache_head[:, :, 0], resp_head[:, :, 0]], axis=2)
    value_rows = jnp.concatenate([cache_head[:, :, 1], resp_head[:, :, 1]], axis=2)
    query_heads = queries.reshape(2, local_reqs, RESP, local_heads, HEAD)
    scores = jnp.einsum(
        "mrshd,mrkd->mrhsk", query_heads, key_rows, preferred_element_type=jnp.float32
    ) * HEAD ** (-0.5)
    allowed = span_mask(cache_lengths, sink_count, window_size)[None, :, None]
    masked = jnp.where(allowed, scores, -jnp.inf)
    row_peak = jnp.max(masked, axis=-1, keepdims=True)
    weights = jnp.exp(masked - row_peak)
    weights = (weights / jnp.sum(weights, axis=-1, keepdims=True)).astype(jnp.bfloat16)
    attended = jnp.einsum(
        "mrhsk,mrkd->mrshd", weights, value_rows, preferred_element_type=jnp.float32
    )
    attended = attended.astype(jnp.bfloat16).reshape(2, local_reqs, RESP, local_heads * HEAD)
    partial_value = jnp.einsum(
        "mrsf,mfd->mrsd", attended, out_proj, preferred_element_type=jnp.float32
    )
    start_slot = tp_index * quarter
    projected = lax.dynamic_slice_in_dim(lax.psum(partial_value, "tp"), start_slot, quarter, axis=2)
    own_residual = lax.dynamic_slice_in_dim(residual, start_slot, quarter, axis=2)
    hidden = own_residual.astype(jnp.float32) + projected
    normed = rms_norm(hidden, norm_gain)
    flat_rows = normed.reshape(2, local_reqs * quarter, normed.shape[3])
    full_head = lax.all_gather(lm_head, "tp", axis=2, tiled=True)
    vocab_rows = full_head.shape[1]
    vocab_start = req_index * vocab_rows
    flat_targets = targets.reshape(-1)
    total_rows = flat_targets.shape[0]
    requests = total_rows // quarter
    logits = jnp.einsum(
        "mnd,mvd->mnv",
        lax.all_gather(flat_rows, "req", axis=1, tiled=True),
        full_head,
        preferred_element_type=jnp.float32,
    )
    block_peak = jnp.max(logits, axis=-1)
    block_total = jnp.sum(jnp.exp(logits - block_peak[..., None]), axis=-1)
    wanted = flat_targets - vocab_start
    target_hits = jnp.arange(vocab_rows, dtype=jnp.int32)[None, None, :] == wanted[None, :, None]
    block_pick = jnp.sum(jnp.where(target_hits, logits, 0.0), axis=-1)
    peak_all = block_peak
    total_all = block_total
    picked_all = block_pick
    peak_all = peak_all.reshape(2, requests, quarter)
    total_all = total_all.reshape(2, requests, quarter)
    picked_all = picked_all.reshape(2, requests, quarter)
    row_order = (
        jnp.zeros((requests,), jnp.int32).at[owner_slot].set(jnp.arange(requests, dtype=jnp.int32))
    )
    owned_reqs = lax.dynamic_slice_in_dim(row_order, req_index * local_reqs, local_reqs)
    vocab_top = lax.pmax(peak_all, "req")
    exp_total, picked = lax.psum((total_all * jnp.exp(peak_all - vocab_top), picked_all), "req")
    logprob = (picked - (vocab_top + jnp.log(exp_total)))[:, owned_reqs]
    lengths_owned = resp_lengths[owned_reqs]
    live_slots = (start_slot + jnp.arange(quarter, dtype=jnp.int32))[None, :] < lengths_owned[
        :, None
    ]
    policy = jnp.where(live_slots, logprob[0], 0.0)
    log_ratio = jnp.where(live_slots, logprob[0] - logprob[1], 0.0)
    policy_total, ratio_total = lax.psum(
        (jnp.sum(policy, axis=1), jnp.sum(log_ratio, axis=1)), "tp"
    )
    counts = lengths_owned.astype(jnp.float32)
    request_scores = jnp.stack([policy_total / counts, ratio_total / counts], axis=1)
    return (policy, request_scores)


def solution(mesh):
    in_specs = (
        P(None, "req", None, "tp"),
        P(None, "req", None, None, None),
        P(None, "req", None, None, None),
        P(None, "req", None, None),
        P(None, "tp", None),
        P(),
        P(None, "req", "tp"),
        P(None, "tp"),
        P(),
        P("req"),
        P(),
        P(),
        P(),
    )
    out_specs = (P("req", "tp"), P("req", None))
    return jax.shard_map(
        per_device, mesh=mesh, in_specs=in_specs, out_specs=out_specs, check_vma=False
    )
```

profile of v0, /device:TPU:8, one launch (start us, length us, event | category | flops | bytes accessed | tf_op | source)
XLA Modules:
  0.0 1325.8 jit_solution(16412632593061100903)
XLA Ops:
  7.2 0.0 copy-start
  7.2 0.0 copy-start.1
  7.2 0.0 copy-start.2
  7.2 0.0 copy-start.3
  7.2 0.0 copy-start.4
  7.2 0.0 copy-start.5
  7.2 0.0 all-reduce.5.cloned.1.call-start
  7.3 1.2 dynamic-slice_bitcast_fusion
  8.5 0.8 dynamic-slice_bitcast_fusion.2
  11.3 0.8 reshape.303
  12.1 0.1 fusion.12
  12.2 0.3 fusion.23
  12.6 0.2 fusion.5
  12.8 0.3 fusion.4
  13.1 0.1 reshape.305
  13.2 0.0 copy-done
  13.2 1.3 convolution_bitcast_fusion
  14.4 0.0 all-reduce.5.cloned.1.call-update
  14.4 0.0 all-gather.4.cloned.1.call-start
  14.5 0.7 all-gather.4.cloned.1.call-update
  15.2 0.0 all-gather.6.cloned.1.call-start
  15.3 60.6 %all-reduce.5.cloned.1.call-done = f32[2,1,32,1536]{3,2,0,1:T(8,128)} async-done(((f32[2,1,32,1536]{3,2,0,1:T(8,128)}), f32[2,1,32,1536]{3,2,0,1:T(8,128)}) %all-reduce.5.cloned.1.call-update) | async-done | bytes 393232 | tf_op jit(solution)/shard_map/psum | solution.py:78
  75.8 0.0 copy-done.1
  75.8 1.0 multiply_reduce_fusion
  76.8 0.0 copy-done.2
  76.9 1.6 multiply_convert_fusion
  78.4 0.0 all-gather.6.cloned.1.call-update
  78.5 0.0 copy-done.3
  78.5 0.1 copy.19
  78.6 0.1 sub.65
  78.7 1.0 scatter_custom_fusion
  79.7 0.6 dynamic_slice.15
  82.2 0.0 copy-done.5
  82.2 0.6 dynamic-slice.5
  83.5 0.8 iota_compare_fusion
  84.3 68.4 %all-gather.4.cloned.1.call-done = bf16[2,1024,1536]{2,1,0:T(8,128)(2,1)} async-done(((bf16[2,1024,384]{2,1,0:T(8,128)(2,1)}), bf16[2,1024,1536]{2,1,0:T(8,128)(2,1)}) %all-gather.4.cloned.1.call-update) | async-done | bytes 6291472 | tf_op jit(solution)/shard_map/all_gather | solution.py:83
  152.7 149.5 %all-gather.6.cloned.1.call-done = bf16[2,1,1024,1536]{3,2,0,1:T(8,128)(2,1)} async-done(((bf16[2,1,8,1536]{3,2,0,1:T(8,128)(2,1)}), bf16[2,1,1024,1536]{3,2,0,1:T(8,128)(2,1)}) %all-gather.6.cloned.1.call-update) | async-done | bytes 6291472 | tf_op jit(solution)/shard_map/all_gather | solution.py:91
  302.2 12.7 fusion.24
  314.9 0.1 reshape.308
  315.0 5.1 exponential_reduce_fusion
  320.1 0.8 reshape.309
  320.9 493.2 %pmax.7 = f32[2,128,8]{2,1,0:T(8,128)S(1)} all-reduce(f32[2,128,8]{2,1,0:T(8,128)S(1)} %reshape.308), channel_id=1, replica_groups=mesh['req'=128,'tp'=4] {'req'}, use_global_device_ids=true, to_apply=%region_8.9 | all-reduce | flops 2048 | bytes 16384 | tf_op jit(solution)/shard_map/pmax | solution.py:110
  814.1 0.1 reshape.307
  814.2 490.9 %all-reduce.1 = (f32[2,128,8]{2,1,0:T(8,128)S(1)}, f32[2,128,8]{2,1,0:T(8,128)S(1)}) all-reduce(f32[2,128,8]{2,1,0:T(8,128)S(1)} %reshape.307, f32[2,128,8]{2,1,0:T(8,128)S(1)} %exponential_multiply_fusion), channel_id=1, replica_groups=mesh['req'=128,'tp'=4] {'req'}, use_global_device_ids=true, to_apply=%region_6.7 | all-reduce | flops 4096 | bytes 32768 | tf_op jit(solution)/shard_map/psum | solution.py:111
  1305.2 1.2 fusion.17
  1306.4 1.7 fusion.22
  1308.1 9.3 all-reduce.2
  1318.7 0.6 pad_maximum_fusion
  (15 shorter events, 0.2 us)
Async XLA Ops:
  7.2 6.0 copy-start
  7.2 68.7 %copy-start.1 = (bf16[2,1,32,1536]{3,2,1,0:T(8,128)(2,1)S(1)}, bf16[2,1,32,1536]{3,2,1,0:T(8,128)(2,1)}, u32[]{:S(2)}) copy-start(bf16[2,1,32,1536]{3,2,1,0:T(8,128)(2,1)} %param.16) | copy-start | bytes 589828
  7.2 69.7 %copy-start.2 = (f32[2,1536]{1,0:T(2,128)S(1)}, f32[2,1536]{1,0:T(2,128)}, u32[]{:S(2)}) copy-start(f32[2,1536]{1,0:T(2,128)} %param.18) | copy-start | bytes 36868
  7.2 71.3 %copy-start.3 = (s32[128,8]{0,1:T(8,128)S(1)}, s32[128,8]{0,1:T(8,128)}, u32[]{:S(2)}) copy-start(s32[128,8]{0,1:T(8,128)} %param.20) | copy-start | bytes 12292
  7.2 71.5 %copy-start.4 = (s32[128]{0:T(128)S(1)}, s32[128]{0:T(128)}, u32[]{:S(2)}) copy-start(s32[128]{0:T(128)} %param.23) | copy-start | bytes 1540
  7.2 75.0 %copy-start.5 = (s32[128]{0:T(128)S(1)}, s32[128]{0:T(128)}, u32[]{:S(2)}) copy-start(s32[128]{0:T(128)} %param.21) | copy-start | bytes 1540
  7.2 68.6 %all-reduce.5.cloned.1.call-start = ((), (), s32[]{:S(2)}) async-start(), calls=%async_computation | async-start | bytes 786432 | tf_op jit(solution)/shard_map/psum | solution.py:78
  14.4 138.2 %all-gather.4.cloned.1.call-start = ((), (), s32[]{:S(2)}) async-start(), calls=%async_computation.1 | async-start | bytes 7864320 | tf_op jit(solution)/shard_map/all_gather | solution.py:83
  15.2 287.0 %all-gather.6.cloned.1.call-start = ((), (), s32[]{:S(2)}) async-start(), calls=%async_computation.2 | async-start | bytes 6340608 | tf_op jit(solution)/shard_map/all_gather | solution.py:91
Sparse Core Ops, SparseCore 0:
  14.6 61.2 all-reduce.4
  78.2 74.4 all-gather.3
  156.4 145.7 all-gather.5
where the time goes:
time: 1330 us
  blocking collectives  993 us (75%)
  waiting for transfers between devices  279 us (21%)
  between operations  19.9 us (1%)
  matrix products  14.6 us (1%)
    pmax x1, blocking collectives, per_device(): vocab_top = lax.pmax(peak_all, 'req')  493 us
    psum x1, blocking collectives, per_device(): lax.psum((total_all * jnp.exp(peak_all - vocab_top), picked_all), 'req')  491 us
    all_gather x1, waiting for transfers between devices, per_device(): lax.all_gather(flat_rows, 'req', axis=1, tiled=True)  149 us
    all_gather x1, waiting for transfers between devices, per_device(): full_head = lax.all_gather(lm_head, 'tp', axis=2, tiled=True)  68.4 us
    psum x1, waiting for transfers between devices, per_device(): lax.psum(partial_value, 'tp')  60.6 us
  transfers between devices with their start and end apart: 3, of which 3 were waited for; matrix products, arithmetic and copies ran while one was open for 0% of the time, Pallas kernels for 0%

commit v1 on v0

--- a/solution.py
+++ b/solution.py
@@ -8,6 +8,24 @@
 KV_HEADS = 2
 RESP = 32
 CACHE = 384
+
+
+def gather_around(array, axis, dim):
+    ways, here, step = (lax.axis_size(axis), lax.axis_index(axis), array.shape[dim])
+    dims = [n * ways if d == dim else n for d, n in enumerate(array.shape)]
+    full = lax.dynamic_update_slice_in_dim(
+        jnp.zeros(dims, array.dtype), array, here * step, axis=dim
+    )
+    going_up = going_down = array
+    for far in range(1, ways // 2 + 1):
+        going_up = lax.ppermute(going_up, axis, [(d, (d + 1) % ways) for d in range(ways)])
+        full = lax.dynamic_update_slice_in_dim(full, going_up, (here - far) % ways * step, axis=dim)
+        if 2 * far < ways:
+            going_down = lax.ppermute(going_down, axis, [(d, (d - 1) % ways) for d in range(ways)])
+            full = lax.dynamic_update_slice_in_dim(
+                full, going_down, (here + far) % ways * step, axis=dim
+            )
+    return full
 
 
 def span_mask(lengths, sink_count, window_size):
@@ -80,7 +98,7 @@
     hidden = own_residual.astype(jnp.float32) + projected
     normed = rms_norm(hidden, norm_gain)
     flat_rows = normed.reshape(2, local_reqs * quarter, normed.shape[3])
-    full_head = lax.all_gather(lm_head, "tp", axis=2, tiled=True)
+    full_head = gather_around(lm_head, "tp", 2)
     vocab_rows = full_head.shape[1]
     vocab_start = req_index * vocab_rows
     flat_targets = targets.reshape(-1)

time: 1330 us -> 1250 us (0.940)
  waiting for transfers between devices: 279 us -> 180 us
    all_gather x1, waiting for transfers between devices: 149 us -> 72 us  [per_device(): lax.all_gather(flat_rows, 'req', axis=1, tiled=True)]
    all_gather x1 -> x0, waiting for transfers between devices: 68.4 us -> none  [per_device(): full_head = lax.all_gather(lm_head, 'tp', axis=2, tiled=True)]
    ppermute x0 -> x3, waiting for transfers between devices: none -> 46.9 us  [the longest x2 46.9 us: gather_around(): lax.ppermute(going_up, axis, [(d, (d + 1) % ways) for d in range(ways)])]
  transfers between devices with their start and end apart: 3 -> 5, of which waited for: 3 -> 4; matrix products, arithmetic and copies ran while one was open for 0% -> 1% of each run, Pallas kernels for 0% -> 0%
where the time goes in v1:
time: 1250 us
  blocking collectives  993 us (79%)
  waiting for transfers between devices  180 us (14%)
  between operations  20.3 us (2%)
  local copies, waits for them, and re-layouts  19.2 us (2%)
  matrix products  14.6 us (1%)
    pmax x1, blocking collectives, per_device(): vocab_top = lax.pmax(peak_all, 'req')  493 us
    psum x1, blocking collectives, per_device(): lax.psum((total_all * jnp.exp(peak_all - vocab_top), picked_all), 'req')  491 us
    all_gather x1, waiting for transfers between devices, per_device(): lax.all_gather(flat_rows, 'req', axis=1, tiled=True)  72 us
    psum x1, waiting for transfers between devices, per_device(): lax.psum(partial_value, 'tp')  61.3 us
    ppermute x2, waiting for transfers between devices, gather_around(): lax.ppermute(going_up, axis, [(d, (d + 1) % ways) for d in range(ways)])  46.9 us
  transfers between devices with their start and end apart: 5, of which 4 were waited for; matrix products, arithmetic and copies ran while one was open for 1% of the time, Pallas kernels for 0%

profile of v1, /device:TPU:8, one launch (start us, length us, event | category | flops | bytes accessed | tf_op | source)
XLA Modules:
  0.0 1249.6 jit_solution(13006740128564873232)
XLA Ops:
  7.2 0.0 copy-start
  7.2 0.0 all-reduce.5.cloned.1.call-start
  7.3 1.2 dynamic-slice_bitcast_fusion
  8.5 0.8 dynamic-slice_bitcast_fusion.2
  11.3 0.8 reshape.303
  12.1 0.1 fusion.12
  12.2 0.3 fusion.23
  12.6 0.2 fusion.5
  12.8 0.3 fusion.4
  13.1 0.1 reshape.305
  13.2 1.3 convolution_bitcast_fusion
  14.4 0.0 all-reduce.5.cloned.1.call-update
  14.4 0.0 all-gather.3.cloned.1.call-start
  14.5 61.3 %all-reduce.5.cloned.1.call-done = f32[2,1,32,1536]{3,2,0,1:T(8,128)} async-done(((f32[2,1,32,1536]{3,2,0,1:T(8,128)}), f32[2,1,32,1536]{3,2,0,1:T(8,128)}) %all-reduce.5.cloned.1.call-update) | async-done | bytes 393232 | tf_op jit(solution)/shard_map/psum | solution.py:96
  75.8 1.0 multiply_reduce_fusion
  76.8 1.6 multiply_convert_fusion
  78.4 0.0 all-gather.3.cloned.1.call-update
  78.4 3.5 collective-permute-start
  81.9 2.4 collective-permute-start.1
  84.3 30.4 %collective-permute-done = bf16[2,1024,384]{2,1,0:T(8,128)(2,1)} collective-permute-done((bf16[2,1024,384]{2,1,0:T(8,128)(2,1)}, bf16[2,1024,384]{2,1,0:T(8,128)(2,1)}, u32[]{:S(2)}, u32[]{:S(2)}) %collective-permute-start) | collective-permute-done | bytes 1572896 | tf_op jit(solution)/shard_map/ppermute | solution.py:21
  114.7 3.6 collective-permute-start.2
  118.4 0.1 copy.19
  118.5 0.1 sub.71
  118.6 0.0 copy-done.5
  118.6 1.0 scatter_custom_fusion
  119.6 0.6 dynamic_slice.15
  122.1 0.6 dynamic-slice.5
  123.4 0.0 copy-start.1
  123.4 3.0 broadcast_in_dim.41
  126.4 1.4 constant_dynamic-update-slice_fusion.3
  127.8 0.8 iota_compare_fusion
  128.6 2.8 constant_dynamic-update-slice_fusion.2
  131.4 0.0 collective-permute-done.1
  131.4 2.8 constant_dynamic-update-slice_fusion.1
  134.2 16.6 %collective-permute-done.2 = bf16[2,1024,384]{2,1,0:T(8,128)(2,1)} collective-permute-done((bf16[2,1024,384]{2,1,0:T(8,128)(2,1)}, bf16[2,1024,384]{2,1,0:T(8,128)(2,1)}, u32[]{:S(2)}, u32[]{:S(2)}) %collective-permute-start.2) | collective-permute-done | bytes 1572896 | tf_op jit(solution)/shard_map/ppermute | solution.py:21
  150.8 2.9 constant_dynamic-update-slice_fusion
  153.7 72.0 %all-gather.3.cloned.1.call-done = bf16[2,1,1024,1536]{3,2,0,1:T(8,128)(2,1)} async-done(((bf16[2,1,8,1536]{3,2,0,1:T(8,128)(2,1)}), bf16[2,1,1024,1536]{3,2,0,1:T(8,128)(2,1)}) %all-gather.3.cloned.1.call-update) | async-done | bytes 6291472 | tf_op jit(solution)/shard_map/all_gather | solution.py:109
  225.7 12.7 %fusion.24 = (f32[2,1024]{1,0:T(2,128)S(1)}, f32[2,1024,1024]{1,2,0:T(8,128)}) fusion(bf16[2,1024,1536]{2,1,0:T(8,128)(2,1)} %constant_dynamic-update-slice_fusion, bf16[2,1,1024,1536]{3,2,0,1:T(8,128)(2,1)} %all-gather.3.cloned.1.call-done), kind=kOutput, calls=%fused_computation.64 | convolution fusion | flops 6444546048 | bytes 20979712 | tf_op jit(solution)/shard_map/mnd,mvd->mnv/dot_general | solution.py:107
  238.4 0.1 reshape.308
  238.5 5.1 exponential_reduce_fusion
  243.6 0.8 reshape.309
  244.4 493.2 %pmax.7 = f32[2,128,8]{2,1,0:T(8,128)S(1)} all-reduce(f32[2,128,8]{2,1,0:T(8,128)S(1)} %reshape.308), channel_id=1, replica_groups=mesh['req'=128,'tp'=4] {'req'}, use_global_device_ids=true, to_apply=%region_8.9 | all-reduce | flops 2048 | bytes 16384 | tf_op jit(solution)/shard_map/pmax | solution.py:128
  737.6 0.1 reshape.307
  737.7 490.9 %all-reduce.1 = (f32[2,128,8]{2,1,0:T(8,128)S(1)}, f32[2,128,8]{2,1,0:T(8,128)S(1)}) all-reduce(f32[2,128,8]{2,1,0:T(8,128)S(1)} %reshape.307, f32[2,128,8]{2,1,0:T(8,128)S(1)} %exponential_multiply_fusion), channel_id=1, replica_groups=mesh['req'=128,'tp'=4] {'req'}, use_global_device_ids=true, to_apply=%region_6.7 | all-reduce | flops 4096 | bytes 32768 | tf_op jit(solution)/shard_map/psum | solution.py:129
  1228.6 1.2 fusion.17
  1229.8 1.7 fusion.22
  1231.6 9.3 all-reduce.2
  1242.2 0.6 pad_maximum_fusion
  (25 shorter events, 0.2 us)
Async XLA Ops:
  7.2 6.0 copy-start
  7.2 68.6 %copy-start.2 = (bf16[2,1,32,1536]{3,2,1,0:T(8,128)(2,1)S(1)}, bf16[2,1,32,1536]{3,2,1,0:T(8,128)(2,1)}, u32[]{:S(2)}) copy-start(bf16[2,1,32,1536]{3,2,1,0:T(8,128)(2,1)} %param.16) | copy-start | bytes 589828
  7.2 69.6 %copy-start.3 = (f32[2,1536]{1,0:T(2,128)S(1)}, f32[2,1536]{1,0:T(2,128)}, u32[]{:S(2)}) copy-start(f32[2,1536]{1,0:T(2,128)} %param.18) | copy-start | bytes 36868
  7.2 111.2 %copy-start.4 = (s32[128,8]{0,1:T(8,128)S(1)}, s32[128,8]{0,1:T(8,128)}, u32[]{:S(2)}) copy-start(s32[128,8]{0,1:T(8,128)} %param.20) | copy-start | bytes 12292
  7.2 111.4 %copy-start.5 = (s32[128]{0:T(128)S(1)}, s32[128]{0:T(128)}, u32[]{:S(2)}) copy-start(s32[128]{0:T(128)} %param.23) | copy-start | bytes 1540
  7.2 114.9 %copy-start.6 = (s32[128]{0:T(128)S(1)}, s32[128]{0:T(128)}, u32[]{:S(2)}) copy-start(s32[128]{0:T(128)} %param.21) | copy-start | bytes 1540
  7.2 68.6 %all-reduce.5.cloned.1.call-start = ((), (), s32[]{:S(2)}) async-start(), calls=%async_computation | async-start | bytes 786432 | tf_op jit(solution)/shard_map/psum | solution.py:96
  14.4 211.2 %all-gather.3.cloned.1.call-start = ((), (), s32[]{:S(2)}) async-start(), calls=%async_computation.1 | async-start | bytes 6340608 | tf_op jit(solution)/shard_map/all_gather | solution.py:109
  78.4 36.2 %collective-permute-start = (bf16[2,1024,384]{2,1,0:T(8,128)(2,1)}, bf16[2,1024,384]{2,1,0:T(8,128)(2,1)}, u32[]{:S(2)}, u32[]{:S(2)}) collective-permute-start(bf16[2,1024,384]{2,1,0:T(8,128)(2,1)} %param.19), channel_id=1, source_target_pairs={{0,1},{1,2},{2,3},{3,0},{4,5},{5,6},{6,7},{7,4},{8,9},{9,10},{10,1... | collective-permute-start | bytes 4718600 | tf_op jit(solution)/shard_map/ppermute | solution.py:21
  81.9 49.5 %collective-permute-start.1 = (bf16[2,1024,384]{2,1,0:T(8,128)(2,1)}, bf16[2,1024,384]{2,1,0:T(8,128)(2,1)}, u32[]{:S(2)}, u32[]{:S(2)}) collective-permute-start(bf16[2,1024,384]{2,1,0:T(8,128)(2,1)} %param.19), channel_id=1, source_target_pairs={{0,3},{1,0},{2,1},{3,2},{4,7},{5,4},{6,5},{7,6},{8,11},{9,8},{10,9... | collective-permute-start | bytes 4718600 | tf_op jit(solution)/shard_map/ppermute | solution.py:24
  114.7 36.1 %collective-permute-start.2 = (bf16[2,1024,384]{2,1,0:T(8,128)(2,1)}, bf16[2,1024,384]{2,1,0:T(8,128)(2,1)}, u32[]{:S(2)}, u32[]{:S(2)}) collective-permute-start(bf16[2,1024,384]{2,1,0:T(8,128)(2,1)} %collective-permute-done), channel_id=1, source_target_pairs={{0,1},{1,2},{2,3},{3,0},{4,5},{5,6},{6,7},{7,4},{8,9},{9,10},{10,1... | collective-permute-start | bytes 4718600 | tf_op jit(solution)/shard_map/ppermute | solution.py:21
  123.4 3.0 copy-start.1
Sparse Core Ops, SparseCore 0:
  14.6 61.1 all-reduce.4
  79.5 146.1 all-gather.2
